TPU v7x, 256 devices: a whole 4x4x8 slice. The times are simulated.
256 devices in a mesh: grp: 16 (over z, core), head: 16 (over y, x).
Axes of the slice: x: 4, y: 4, z: 8, core: 2. Of those that a mesh axis runs over, the one named last changes fastest.
Arguments:
- query_rows: bfloat16 [256, 128, 2048], P(('grp', 'head')), may hold values from -6 to 6
- key_rows: bfloat16 [256, 128, 2048], P(('grp', 'head')), may hold values from -6 to 6
- value_rows: bfloat16 [256, 128, 2048], P(('grp', 'head')), may hold values from -6 to 6
- log_decay: bfloat16 [256, 128, 2048], P(('grp', 'head')), may hold values from -1.5 to 0, as said below
- beta_logit: bfloat16 [256, 128, 16], P(('grp', 'head')), may hold values from -6 to 6
- out_grad: bfloat16 [256, 128, 2048], P(('grp', 'head')), may hold values from -6 to 6
- fork_state: float32 [8, 16, 128, 128], P(None, 'head'), may hold values from -6 to 6
- branch_prompt: int32 [256], replicated, may hold values from 0 to 7, as said below
- valid_len: int32 [256], replicated, may hold values from 32 to 128, as said below
Outputs:
- grad_query: bfloat16 [256, 128, 2048], P(('grp', 'head'))
- grad_key: bfloat16 [256, 128, 2048], P(('grp', 'head'))
- grad_value: bfloat16 [256, 128, 2048], P(('grp', 'head'))
- grad_decay: bfloat16 [256, 128, 2048], P(('grp', 'head'))
- grad_beta: bfloat16 [256, 128, 16], P(('grp', 'head'))
- grad_fork: float32 [8, 16, 128, 128], P(None, 'head')
Inputs may be any that keep to these rules, and one draw needn't show every extreme that they name: `log_decay`: never positive; a few tokens of each branch lose a large share of every channel at once. `branch_prompt`: every prompt has at least one branch. A branch counts its first valid_len tokens; some branch uses all 128.
All inputs are finite; a program needn't handle non-finite values.
Results may differ from a plain program's by a relative error of at most 0.0015.
Values may be sent and summed in bfloat16 or wider, within the bound.
A program may use at most 64 MiB of HBM per device.

v0:
```python
from functools import partial
import jax
import jax.numpy as jnp
from jax import lax
from jax.sharding import PartitionSpec as P


def decay_forward(query_in, key_in, value_in, decay_in, beta_in, state_in, keep_mask, block_len):
    head_dim = query_in.shape[-1]
    upper_limit = lax.Precision.HIGHEST
    unit_query = (
        query_in
        * lax.rsqrt(jnp.sum(query_in * query_in, axis=-1, keepdims=True) + 1e-06)
        * head_dim ** (-0.5)
    )
    unit_key = key_in * lax.rsqrt(jnp.sum(key_in * key_in, axis=-1, keepdims=True) + 1e-06)
    beta_value = jax.nn.sigmoid(beta_in) * keep_mask[None, :]
    decay_value = decay_in * keep_mask[None, :, None]
    token_positions = jnp.arange(block_len, dtype=jnp.int32)
    lower_strict = (token_positions[:, None] > token_positions[None, :]).astype(jnp.float32)
    lower_closed = (token_positions[:, None] >= token_positions[None, :]).astype(jnp.float32)
    identity_block = jnp.eye(block_len, dtype=jnp.float32)
    cum_decay = jnp.cumsum(decay_value, axis=1)
    growth = jnp.exp(cum_decay)
    shrink = jnp.exp(-cum_decay)
    key_forward_rows = unit_key * growth
    key_earlier_rows = unit_key * shrink
    query_forward_rows = unit_query * growth
    coupling = (
        jnp.einsum("htk,hsk->hts", key_forward_rows, key_earlier_rows, precision=upper_limit)
        * beta_value[:, :, None]
        * lower_strict
    )
    attend_scores = (
        jnp.einsum("htk,hsk->hts", query_forward_rows, key_earlier_rows, precision=upper_limit)
        * lower_closed
    )
    target_output = beta_value[:, :, None] * (
        value_in - jnp.einsum("led,ldf->lef", key_forward_rows, state_in, precision=upper_limit)
    )
    state_update = jax.scipy.linalg.solve_triangular(
        identity_block + coupling, target_output, lower=True, unit_diagonal=True
    )
    output_block_rows = jnp.einsum(
        "led,ldf->lef", query_forward_rows, state_in, precision=upper_limit
    ) + jnp.einsum("ifj,ijo->ifo", attend_scores, state_update, precision=upper_limit)
    outputs = [output_block_rows]
    return jnp.concatenate(outputs, axis=1)


def branch_backward(
    query_rows, key_rows, value_rows, log_decay, out_grad, beta_logit, states, valid_rows, block_len
):
    count, window_len, row_width = query_rows.shape
    heads_here = states.shape[1]
    head_dim = states.shape[-1]

    def split_heads(array_in):
        return (
            array_in.astype(jnp.float32)
            .reshape(count, window_len, heads_here, head_dim)
            .transpose(0, 2, 1, 3)
        )

    def join_heads(array_in):
        return (
            array_in.transpose(0, 2, 1, 3)
            .reshape(count, window_len, row_width)
            .astype(jnp.bfloat16)
        )

    keep_mask = (jnp.arange(window_len, dtype=jnp.int32)[None, :] < valid_rows[:, None]).astype(
        jnp.float32
    )
    beta_in = beta_logit.astype(jnp.float32).transpose(0, 2, 1)
    mapped = jax.vmap(partial(decay_forward, block_len=block_len))

    def forward_all(query_in, key_in, value_in, decay_in, beta_all, state_all):
        return mapped(query_in, key_in, value_in, decay_in, beta_all, state_all, keep_mask)

    outputs, pullback = jax.vjp(
        forward_all,
        split_heads(query_rows),
        split_heads(key_rows),
        split_heads(value_rows),
        split_heads(log_decay),
        beta_in,
        states,
    )
    cotangent = split_heads(out_grad) * keep_mask[:, None, :, None]
    grad_q, grad_k, grad_v, grad_g, grad_b, grad_s = pullback(cotangent)
    gradients = (
        join_heads(grad_q),
        join_heads(grad_k),
        join_heads(grad_v),
        join_heads(grad_g),
        grad_b.transpose(0, 2, 1).astype(jnp.bfloat16),
    )
    return (gradients, grad_s)


def per_device(
    query_rows,
    key_rows,
    value_rows,
    log_decay,
    beta_logit,
    out_grad,
    fork_state,
    branch_prompt,
    valid_len,
):
    upper_limit = lax.Precision.HIGHEST
    local_count = query_rows.shape[0]
    head_count = lax.axis_size("head")
    group_size = local_count * head_count
    group_first = lax.axis_index("grp") * group_size
    prompt_count = fork_state.shape[0]
    prompt_ids = jnp.arange(prompt_count, dtype=jnp.int32)
    window_len = query_rows.shape[1]
    group_prompt = lax.dynamic_slice_in_dim(branch_prompt, group_first, group_size)
    group_onehot = (group_prompt[:, None] == prompt_ids[None, :]).astype(jnp.float32)
    group_states = jnp.einsum("bp,phij->bhij", group_onehot, fork_state, precision=upper_limit)
    arrived = (
        lax.all_to_all(query_rows, "head", split_axis=2, concat_axis=0, tiled=True),
        lax.all_to_all(key_rows, "head", split_axis=2, concat_axis=0, tiled=True),
        lax.all_to_all(value_rows, "head", split_axis=2, concat_axis=0, tiled=True),
        lax.all_to_all(log_decay, "head", split_axis=2, concat_axis=0, tiled=True),
        lax.all_to_all(out_grad, "head", split_axis=2, concat_axis=0, tiled=True),
        lax.all_to_all(beta_logit, "head", split_axis=2, concat_axis=0, tiled=True),
    )
    group_len = lax.dynamic_slice_in_dim(valid_len, group_first, group_size)
    gradients, state_grad = branch_backward(
        arrived[0],
        arrived[1],
        arrived[2],
        arrived[3],
        arrived[4],
        arrived[5],
        group_states,
        group_len,
        window_len,
    )
    prompt_grad = jnp.einsum("bp,bhij->phij", group_onehot, state_grad, precision=upper_limit)
    results = (
        lax.all_to_all(gradients[0], "head", split_axis=0, concat_axis=2, tiled=True),
        lax.all_to_all(gradients[1], "head", split_axis=0, concat_axis=2, tiled=True),
        lax.all_to_all(gradients[2], "head", split_axis=0, concat_axis=2, tiled=True),
        lax.all_to_all(gradients[3], "head", split_axis=0, concat_axis=2, tiled=True),
        lax.all_to_all(gradients[4], "head", split_axis=0, concat_axis=2, tiled=True),
    )
    grad_fork = lax.psum(prompt_grad, "grp")
    return (results[0], results[1], results[2], results[3], results[4], grad_fork)


def solution(mesh):
    return jax.shard_map(
        per_device,
        mesh=mesh,
        in_specs=(
            P(("grp", "head"), None, None),
            P(("grp", "head"), None, None),
            P(("grp", "head"), None, None),
            P(("grp", "head"), None, None),
            P(("grp", "head"), None, None),
            P(("grp", "head"), None, None),
            P(None, "head", None, None),
            P(),
            P(),
        ),
        out_specs=(
            P(("grp", "head"), None, None),
            P(("grp", "head"), None, None),
            P(("grp", "head"), None, None),
            P(("grp", "head"), None, None),
            P(("grp", "head"), None, None),
            P(None, "head", None, None),
        ),
        check_vma=False,
    )
```

profile of v0, /device:TPU:1, one launch (start us, length us, event | category | flops | bytes accessed | tf_op | source)
XLA Modules:
  0.0 567.9 jit_solution(9979392489376102869)
XLA Ops:
  7.2 1.3 copy.205
  8.5 7.6 %all-to-all-start.3 = ((bf16[1,128,16]{1,0,2:T(2,128)(2,1)}), bf16[1,128,16]{1,0,2:T(2,128)(2,1)S(1)}, u32[]{:S(2)}, u32[]{:S(2)}) async-start(bf16[1,128,16]{1,0,2:T(2,128)(2,1)} %copy.205), calls=%async_computation.3 | async-start | bytes 16384 | tf_op jit(solution)/shard_map/all_to_all | solution.py:130
  16.9 2.4 copy.217
  19.8 11.5 %reduce.13 = bf16[2048,128]{1,0:T(8,128)(2,1)S(1)} reduce(bf16[2048,1,128]{2,1,0:T(2,128)(2,1)S(1)} %bitcast.201, bf16[]{:T(256)} %broadcast.315), dimensions={1}, to_apply=%bitcast.156.reduce_sub_computation | reduce | bytes 1048578
  32.3 7.0 %all-to-all-start.5 = ((bf16[16,2,8192]{2,1,0:T(2,128)(2,1)}), bf16[16,2,8192]{2,1,0:T(2,128)(2,1)S(1)}, u32[]{:S(2)}, u32[]{:S(2)}) async-start(bf16[16,2,8192]{2,1,0:T(2,128)(2,1)} %reshape.506), calls=%async_computation.5 | async-start | bytes 1048576 | tf_op jit(solution)/shard_map/all_to_all | solution.py:125
  40.0 11.5 %reduce.10 = bf16[2048,128]{1,0:T(8,128)(2,1)S(1)} reduce(bf16[2048,1,128]{2,1,0:T(2,128)(2,1)S(1)} %bitcast.205, bf16[]{:T(256)} %broadcast.315), dimensions={1}, to_apply=%bitcast.158.reduce_sub_computation | reduce | bytes 1048578
  53.4 11.5 %reduce.11 = bf16[2048,128]{1,0:T(8,128)(2,1)S(1)} reduce(bf16[2048,1,128]{2,1,0:T(2,128)(2,1)S(1)} %bitcast.206, bf16[]{:T(256)} %broadcast.315), dimensions={1}, to_apply=%bitcast.162.reduce_sub_computation | reduce | bytes 1048578
  66.7 11.7 %reduce.12 = bf16[2048,128]{1,0:T(8,128)(2,1)S(1)} reduce(bf16[2048,1,128]{2,1,0:T(2,128)(2,1)S(1)} %bitcast.207, bf16[]{:T(256)} %broadcast.315), dimensions={1}, to_apply=%bitcast.160.reduce_sub_computation | reduce | bytes 1048578
  80.3 11.5 %reduce.14 = bf16[2048,128]{1,0:T(8,128)(2,1)S(1)} reduce(bf16[2048,1,128]{2,1,0:T(2,128)(2,1)S(1)} %bitcast.202, bf16[]{:T(256)} %broadcast.315), dimensions={1}, to_apply=%bitcast.164.reduce_sub_computation | reduce | bytes 1048578
  92.9 1.8 fusion.41
  94.7 6.7 %all-to-all-start.1 = ((bf16[16,2,8192]{2,1,0:T(2,128)(2,1)}), bf16[16,2,8192]{2,1,0:T(2,128)(2,1)S(1)}, u32[]{:S(2)}, u32[]{:S(2)}) async-start(bf16[16,2,8192]{2,1,0:T(2,128)(2,1)} %reshape.508), calls=%async_computation.1 | async-start | bytes 1048576 | tf_op jit(solution)/shard_map/all_to_all | solution.py:126
  102.0 1.1 bitcast_convert_fusion.3
  103.1 7.9 %all-to-all-done.1 = bf16[16,2,8192]{2,1,0:T(2,128)(2,1)S(1)} async-done(((bf16[16,2,8192]{2,1,0:T(2,128)(2,1)}), bf16[16,2,8192]{2,1,0:T(2,128)(2,1)S(1)}, u32[]{:S(2)}, u32[]{:S(2)}) %all-to-all-start.1) | async-done | bytes 524320 | tf_op jit(solution)/shard_map/all_to_all | solution.py:126
  111.0 4.6 all-to-all-start.2
  116.3 1.1 bitcast_convert_fusion.2
  117.6 7.1 %all-to-all-done.2 = bf16[16,2,8192]{2,1,0:T(2,128)(2,1)} async-done(((bf16[16,2,8192]{2,1,0:T(2,128)(2,1)}), bf16[16,2,8192]{2,1,0:T(2,128)(2,1)}, u32[]{:S(2)}, u32[]{:S(2)}) %all-to-all-start.2) | async-done | bytes 524320 | tf_op jit(solution)/shard_map/all_to_all | solution.py:128
  124.7 4.2 all-to-all-start
  129.0 2.2 reshape.513
  131.2 1.9 bitcast_convert_fusion
  133.1 1.7 copy.200
  134.8 1.3 fusion.27
  136.2 1.6 copy.201
  137.8 1.5 multiply_multiply_fusion.2
  140.2 1.9 fusion.21
  143.5 157.8 %custom-call.7 = f32[16,1,128,128]{2,3,1,0:T(8,128)} custom-call(f32[16,1,128,128]{3,2,1,0:T(8,128)S(1)} %add_bitcast_fusion), custom_call_target="InvertDiagBlocksLowerTriangular" | custom-call | tf_op jit(solution)/shard_map/jvp(vmap(jit(_solve_triangular)))/triangular_solve | solution.py:41
  301.3 6.6 %all-to-all-start.4 = ((bf16[16,2,8192]{2,1,0:T(2,128)(2,1)}), bf16[16,2,8192]{2,1,0:T(2,128)(2,1)}, u32[]{:S(2)}, u32[]{:S(2)}) async-start(bf16[16,2,8192]{2,1,0:T(2,128)(2,1)} %reshape.514), calls=%async_computation.4 | async-start | bytes 1048576 | tf_op jit(solution)/shard_map/all_to_all | solution.py:127
  307.9 2.2 reshape.511
  310.1 2.0 bitcast_convert_fusion.1
  312.1 1.7 copy.194
  313.8 1.4 fusion.28
  315.2 1.6 copy.221
  317.0 3.6 reshape.515
  320.6 2.1 copy.210
  322.7 2.3 copy.211
  325.0 3.4 convolution_multiply_fusion
  328.4 1.2 convolution_bitcast_fusion
  330.2 2.2 convolution_subtract_fusion
  332.4 2.2 fusion.16
  334.6 3.5 multiply_reduce_fusion.1
  339.2 3.2 convolution_multiply_fusion.1
  342.4 2.4 fusion.37
  344.8 3.3 multiply_reduce_fusion
  348.8 6.4 %all-to-all-start.10 = ((bf16[16,128,1]{1,2,0:T(2,128)(2,1)}), bf16[16,128,1]{1,2,0:T(2,128)(2,1)S(1)}, u32[]{:S(2)}, u32[]{:S(2)}) async-start(bf16[16,128,1]{1,2,0:T(2,128)(2,1)} %copy.235), calls=%async_computation.10 | async-start | bytes 16384 | tf_op jit(solution)/shard_map/all_to_all | solution.py:150
  355.3 4.2 fusion.31
  361.0 2.3 convolution_add_fusion.3
  363.4 1.3 convolution_add_fusion.2
  365.0 4.3 multiply_reduce_fusion.2
  369.3 2.7 copy.230
  372.0 3.5 multiply_convert_fusion
  376.4 6.7 %all-to-all-start.9 = ((bf16[16,128,128]{2,1,0:T(8,128)(2,1)}), bf16[16,128,128]{2,1,0:T(8,128)(2,1)}, u32[]{:S(2)}, u32[]{:S(2)}) async-start(bf16[16,128,128]{2,1,0:T(8,128)(2,1)} %copy.231), calls=%async_computation.9 | async-start | bytes 1048576 | tf_op jit(solution)/shard_map/all_to_all | solution.py:149
  383.1 4.0 fusion.4
  387.1 5.0 all-to-all-done.9
  392.2 13.4 %all_to_all.144 = bf16[16,128,128]{1,2,0:T(8,128)(2,1)} all-to-all(bf16[16,128,128]{1,2,0:T(8,128)(2,1)} %get-tuple-element.45), channel_id=1, replica_groups=mesh['grp'=16,'head'=16] {'head'}, dimensions={0} | all-to-all | bytes 1048576 | tf_op jit(solution)/shard_map/all_to_all | solution.py:146
  405.5 4.5 all-to-all-start.7
  410.0 3.3 fusion.8
  413.3 5.7 %all-to-all-done.7 = bf16[16,128,128]{1,2,0:T(8,128)(2,1)} async-done(((bf16[16,128,128]{1,2,0:T(8,128)(2,1)}), bf16[16,128,128]{1,2,0:T(8,128)(2,1)}, u32[]{:S(2)}, u32[]{:S(2)}) %all-to-all-start.7) | async-done | bytes 524320 | tf_op jit(solution)/shard_map/all_to_all | solution.py:147
  419.0 4.2 all-to-all-start.8
  423.4 3.4 fusion
  427.2 1.3 convolution_bitcast_fusion.1
  429.1 121.8 %all-reduce.2.cloned.1.call-done = f32[8,1,128,128]{3,0,2,1:T(8,128)} async-done(((f32[8,1,128,128]{3,0,2,1:T(8,128)}), f32[8,1,128,128]{3,0,2,1:T(8,128)}) %all-reduce.2.cloned.1.call-update) | async-done | bytes 524304 | tf_op jit(solution)/shard_map/psum | solution.py:152
  550.9 1.9 copy.245
  552.8 1.3 copy.232
  556.2 2.0 copy.242
  558.2 1.3 copy.229
  (104 shorter events, 22.6 us)
Async XLA Ops:
  7.2 85.7 %copy-start = (f32[8,1,128,128]{3,2,1,0:T(8,128)S(1)}, f32[8,1,128,128]{3,2,1,0:T(8,128)}, u32[]{:S(2)}) copy-start(f32[8,1,128,128]{3,2,1,0:T(8,128)} %param.17) | copy-start | bytes 1572868
  8.5 23.7 %all-to-all-start.3 = ((bf16[1,128,16]{1,0,2:T(2,128)(2,1)}), bf16[1,128,16]{1,0,2:T(2,128)(2,1)S(1)}, u32[]{:S(2)}, u32[]{:S(2)}) async-start(bf16[1,128,16]{1,0,2:T(2,128)(2,1)} %copy.205), calls=%async_computation.3 | async-start | bytes 16384 | tf_op jit(solution)/shard_map/all_to_all | solution.py:130
  16.1 0.7 copy-start.28
  32.2 7.0 %copy-start.24 = (bf16[1,128,2048]{2,1,0:T(8,128)(2,1)S(1)}, bf16[1,128,2048]{2,1,0:T(8,128)(2,1)}, u32[]{:S(2)}) copy-start(bf16[1,128,2048]{2,1,0:T(8,128)(2,1)} %param.12) | copy-start | bytes 1572868
  32.3 62.4 %all-to-all-start.5 = ((bf16[16,2,8192]{2,1,0:T(2,128)(2,1)}), bf16[16,2,8192]{2,1,0:T(2,128)(2,1)S(1)}, u32[]{:S(2)}, u32[]{:S(2)}) async-start(bf16[16,2,8192]{2,1,0:T(2,128)(2,1)} %reshape.506), calls=%async_computation.5 | async-start | bytes 1048576 | tf_op jit(solution)/shard_map/all_to_all | solution.py:125
  51.5 1.1 copy-start.25
  64.9 1.1 copy-start.26
  78.5 0.9 copy-start.29
  78.5 1.1 copy-start.27
  94.7 16.4 %all-to-all-start.1 = ((bf16[16,2,8192]{2,1,0:T(2,128)(2,1)}), bf16[16,2,8192]{2,1,0:T(2,128)(2,1)S(1)}, u32[]{:S(2)}, u32[]{:S(2)}) async-start(bf16[16,2,8192]{2,1,0:T(2,128)(2,1)} %reshape.508), calls=%async_computation.1 | async-start | bytes 1048576 | tf_op jit(solution)/shard_map/all_to_all | solution.py:126
  111.0 13.7 %all-to-all-start.2 = ((bf16[16,2,8192]{2,1,0:T(2,128)(2,1)}), bf16[16,2,8192]{2,1,0:T(2,128)(2,1)}, u32[]{:S(2)}, u32[]{:S(2)}) async-start(bf16[16,2,8192]{2,1,0:T(2,128)(2,1)} %reshape.512), calls=%async_computation.2 | async-start | bytes 1048576 | tf_op jit(solution)/shard_map/all_to_all | solution.py:128
  124.7 176.6 %all-to-all-start = ((bf16[16,2,8192]{2,1,0:T(2,128)(2,1)}), bf16[16,2,8192]{2,1,0:T(2,128)(2,1)}, u32[]{:S(2)}, u32[]{:S(2)}) async-start(bf16[16,2,8192]{2,1,0:T(2,128)(2,1)} %reshape.510), calls=%async_computation | async-start | bytes 1048576 | tf_op jit(solution)/shard_map/all_to_all | solution.py:129
  137.7 1.5 copy-start.11
  139.2 1.0 copy-start.2
  139.2 2.9 copy-start.4
  142.2 1.0 copy-start.16
  301.3 15.7 %all-to-all-start.4 = ((bf16[16,2,8192]{2,1,0:T(2,128)(2,1)}), bf16[16,2,8192]{2,1,0:T(2,128)(2,1)}, u32[]{:S(2)}, u32[]{:S(2)}) async-start(bf16[16,2,8192]{2,1,0:T(2,128)(2,1)} %reshape.514), calls=%async_computation.4 | async-start | bytes 1048576 | tf_op jit(solution)/shard_map/all_to_all | solution.py:127
  328.4 1.2 copy-start.5
  328.4 1.5 copy-start.10
  328.4 1.8 copy-start.22
  330.2 2.2 copy-start.19
  342.4 2.4 copy-start.17
  348.8 27.6 %all-to-all-start.10 = ((bf16[16,128,1]{1,2,0:T(2,128)(2,1)}), bf16[16,128,1]{1,2,0:T(2,128)(2,1)S(1)}, u32[]{:S(2)}, u32[]{:S(2)}) async-start(bf16[16,128,1]{1,2,0:T(2,128)(2,1)} %copy.235), calls=%async_computation.10 | async-start | bytes 16384 | tf_op jit(solution)/shard_map/all_to_all | solution.py:150
  355.2 4.2 copy-start.8
  355.2 4.2 copy-start.15
  359.5 1.2 copy-start.3
  359.5 1.5 copy-start.21
  361.0 2.3 copy-start.6
  361.0 2.3 copy-start.20
  363.4 1.4 copy-start.13
  363.4 1.6 copy-start.12
  364.7 4.5 copy-start.14
  376.4 15.8 %all-to-all-start.9 = ((bf16[16,128,128]{2,1,0:T(8,128)(2,1)}), bf16[16,128,128]{2,1,0:T(8,128)(2,1)}, u32[]{:S(2)}, u32[]{:S(2)}) async-start(bf16[16,128,128]{2,1,0:T(8,128)(2,1)} %copy.231), calls=%async_computation.9 | async-start | bytes 1048576 | tf_op jit(solution)/shard_map/all_to_all | solution.py:149
  392.2 17.9 %copy-start.9 = (f32[16,1,128,128]{2,3,0,1:T(8,128)S(1)}, f32[16,1,128,128]{2,3,0,1:T(8,128)}, u32[]{:S(2)}) copy-start(f32[16,1,128,128]{2,3,0,1:T(8,128)} %get-tuple-element.46) | copy-start | bytes 3145732
  405.5 13.5 %all-to-all-start.7 = ((bf16[16,128,128]{1,2,0:T(8,128)(2,1)}), bf16[16,128,128]{1,2,0:T(8,128)(2,1)}, u32[]{:S(2)}, u32[]{:S(2)}) async-start(bf16[16,128,128]{1,2,0:T(8,128)(2,1)} %get-tuple-element.44), calls=%async_computation.7 | async-start | bytes 1048576 | tf_op jit(solution)/shard_map/all_to_all | solution.py:147
  410.0 13.3 %copy-start.18 = (f32[16,128,128]{2,1,0:T(8,128)S(1)}, f32[16,128,128]{2,1,0:T(8,128)}, u32[]{:S(2)}) copy-start(f32[16,128,128]{2,1,0:T(8,128)} %get-tuple-element.50) | copy-start | bytes 3145732
  413.3 10.0 %copy-start.7 = (f32[16,1,128,128]{2,3,0,1:T(8,128)S(1)}, f32[16,1,128,128]{2,3,0,1:T(8,128)}, u32[]{:S(2)}) copy-start(f32[16,1,128,128]{2,3,0,1:T(8,128)} %copy-done.4) | copy-start | bytes 3145732
  419.0 139.2 %all-to-all-start.8 = ((bf16[16,128,128]{2,1,0:T(8,128)(2,1)}), bf16[16,128,128]{2,1,0:T(8,128)(2,1)}, u32[]{:S(2)}, u32[]{:S(2)}) async-start(bf16[16,128,128]{2,1,0:T(8,128)(2,1)} %get-tuple-element.43), calls=%async_computation.8 | async-start | bytes 1048576 | tf_op jit(solution)/shard_map/all_to_all | solution.py:148
  423.3 127.6 %all-reduce.2.cloned.1.call-start = ((), (), s32[]{:S(2)}) async-start(), calls=%async_computation.11 | async-start | bytes 1048576 | tf_op jit(solution)/shard_map/psum | solution.py:152
  554.1 1.0 copy-start.23
  559.6 1.0 copy-start.1
Sparse Core Ops, SparseCore 0:
  428.6 122.2 all-reduce.1
where the time goes:
time: 575 us; the launch traced here: 568 us
  other arithmetic  234 us (41%)
  waiting for transfers between devices  148 us (26%)
  starting transfers between devices  58.7 us (10%)
  local copies, waits for them, and re-layouts  51.4 us (9%)
  matrix products  47.3 us (8%)
  between operations  15.1 us (3%)
  blocking collectives  13.4 us (2%)
    another operation x4, other arithmetic, decay_forward(): jax.scipy.linalg.solve_triangular(identity_block + coupling, target_outpu...  158 us
    psum x1, waiting for transfers between devices, per_device(): grad_fork = lax.psum(prompt_grad, 'grp')  122 us
    unnamed x5, other arithmetic  57.9 us
    unnamed x83, local copies, waits for them, and re-layouts  32.9 us
    all_to_all x1, blocking collectives, per_device(): lax.all_to_all(gradients[0], 'head', split_axis=0, concat_axis=2, tiled=T...  13.4 us
  transfers between devices with their start and end apart: 11, of which 6 were waited for; matrix products, arithmetic and copies ran while one was open for 52% of the time, Pallas kernels for 0%

commit v1 on v0

--- a/solution.py
+++ b/solution.py
@@ -3,6 +3,17 @@
 import jax.numpy as jnp
 from jax import lax
 from jax.sharding import PartitionSpec as P
+
+
+def links_switch(row_data):
+    total_devices = lax.axis_size("grp")
+    mid_arr = row_data
+    for nth in [dd for dd in (1, 2, 4, 8, 16) if dd < total_devices]:
+        seen = []
+        for it in range(total_devices):
+            seen.append((it, it ^ nth))
+        mid_arr = mid_arr + lax.ppermute(mid_arr, axis_name="grp", perm=seen)
+    return mid_arr
 
 
 def decay_forward(query_in, key_in, value_in, decay_in, beta_in, state_in, keep_mask, block_len):
@@ -149,7 +160,7 @@
         lax.all_to_all(gradients[3], "head", split_axis=0, concat_axis=2, tiled=True),
         lax.all_to_all(gradients[4], "head", split_axis=0, concat_axis=2, tiled=True),
     )
-    grad_fork = lax.psum(prompt_grad, "grp")
+    grad_fork = links_switch(prompt_grad)
     return (results[0], results[1], results[2], results[3], results[4], grad_fork)
 
 

time: 575 us -> 477 us (0.83)
  waiting for transfers between devices: 148 us -> 49 us
  starting transfers between devices: 58.7 us -> 80.1 us
  between operations: 15.1 us -> 1.67 us
  blocking collectives: 13.4 us -> 0 us
  matrix products: 47.3 us -> 54.3 us
    psum x1 -> x0, waiting for transfers between devices: 122 us -> none  [per_device(): grad_fork = lax.psum(prompt_grad, 'grp')]
    ppermute x0 -> x4, waiting for transfers between devices: none -> 21.1 us  [links_switch(): mid_arr = mid_arr + lax.ppermute(mid_arr, axis_name='grp', perm=seen)]
    ppermute x0 -> x4, starting transfers between devices: none -> 15.9 us  [links_switch(): mid_arr = mid_arr + lax.ppermute(mid_arr, axis_name='grp', perm=seen)]
    all_to_all x1 -> x0, blocking collectives: 13.4 us -> none  [per_device(): lax.all_to_all(gradients[0], 'head', split_axis=0, concat_axis=2, tiled=T...]
    unnamed x83 -> x81, local copies, waits for them, and re-layouts: 32.9 us -> 30.2 us
  transfers between devices with their start and end apart: 11 -> 15, of which waited for: 6 -> 8; matrix products, arithmetic and copies ran while one was open for 52% -> 63% of each run, Pallas kernels for 0% -> 0%
where the time goes in v1:
time: 477 us; the launch traced here: 471 us
  other arithmetic  237 us (50%)
  starting transfers between devices  80.1 us (17%)
  matrix products  54.3 us (11%)
  waiting for transfers between devices  49 us (10%)
  local copies, waits for them, and re-layouts  48.5 us (10%)
    another operation x4, other arithmetic, decay_forward(): jax.scipy.linalg.solve_triangular(identity_block + coupling, target_outpu...  158 us
    unnamed x5, other arithmetic  57.8 us
    unnamed x81, local copies, waits for them, and re-layouts  30.2 us
    ppermute x4, waiting for transfers between devices, links_switch(): mid_arr = mid_arr + lax.ppermute(mid_arr, axis_name='grp', perm=seen)  21.1 us
    ppermute x4, starting transfers between devices, links_switch(): mid_arr = mid_arr + lax.ppermute(mid_arr, axis_name='grp', perm=seen)  15.9 us
    dot_general x3, matrix products, decay_forward(): jnp.einsum('led,ldf->lef', key_forward_rows, state_in, precision=upper_li...  10.9 us
    another operation x3, matrix products, decay_forward(): jax.scipy.linalg.solve_triangular(identity_block + coupling, target_outpu...  10.2 us
  transfers between devices with their start and end apart: 15, of which 8 were waited for; matrix products, arithmetic and copies ran while one was open for 63% of the time, Pallas kernels for 0%

profile of v1, /device:TPU:1, one launch (start us, length us, event | category | flops | bytes accessed | tf_op | source)
XLA Modules:
  0.0 470.7 jit_solution(14486415102797818273)
XLA Ops:
  2.0 7.6 %all-to-all-start.3 = ((bf16[1,128,16]{1,0,2:T(2,128)(2,1)}), bf16[1,128,16]{1,0,2:T(2,128)(2,1)S(1)}, u32[]{:S(2)}, u32[]{:S(2)}) async-start(bf16[1,128,16]{1,0,2:T(2,128)(2,1)} %copy.205), calls=%async_computation.3 | async-start | bytes 16384 | tf_op jit(solution)/shard_map/all_to_all | solution.py:141
  10.4 2.4 copy.217
  13.3 11.5 %reduce.13 = bf16[2048,128]{1,0:T(8,128)(2,1)S(1)} reduce(bf16[2048,1,128]{2,1,0:T(2,128)(2,1)S(1)} %bitcast.201, bf16[]{:T(256)} %broadcast.315), dimensions={1}, to_apply=%bitcast.156.reduce_sub_computation | reduce | bytes 1048578
  25.7 7.3 %all-to-all-start.5 = ((bf16[16,2,8192]{2,1,0:T(2,128)(2,1)}), bf16[16,2,8192]{2,1,0:T(2,128)(2,1)S(1)}, u32[]{:S(2)}, u32[]{:S(2)}) async-start(bf16[16,2,8192]{2,1,0:T(2,128)(2,1)} %reshape.506), calls=%async_computation.5 | async-start | bytes 1048576 | tf_op jit(solution)/shard_map/all_to_all | solution.py:136
  33.8 11.5 %reduce.10 = bf16[2048,128]{1,0:T(8,128)(2,1)S(1)} reduce(bf16[2048,1,128]{2,1,0:T(2,128)(2,1)S(1)} %bitcast.205, bf16[]{:T(256)} %broadcast.315), dimensions={1}, to_apply=%bitcast.158.reduce_sub_computation | reduce | bytes 1048578
  47.1 11.5 %reduce.11 = bf16[2048,128]{1,0:T(8,128)(2,1)S(1)} reduce(bf16[2048,1,128]{2,1,0:T(2,128)(2,1)S(1)} %bitcast.206, bf16[]{:T(256)} %broadcast.315), dimensions={1}, to_apply=%bitcast.162.reduce_sub_computation | reduce | bytes 1048578
  60.5 11.7 %reduce.12 = bf16[2048,128]{1,0:T(8,128)(2,1)S(1)} reduce(bf16[2048,1,128]{2,1,0:T(2,128)(2,1)S(1)} %bitcast.207, bf16[]{:T(256)} %broadcast.315), dimensions={1}, to_apply=%bitcast.160.reduce_sub_computation | reduce | bytes 1048578
  74.0 11.5 %reduce.14 = bf16[2048,128]{1,0:T(8,128)(2,1)S(1)} reduce(bf16[2048,1,128]{2,1,0:T(2,128)(2,1)S(1)} %bitcast.202, bf16[]{:T(256)} %broadcast.315), dimensions={1}, to_apply=%bitcast.164.reduce_sub_computation | reduce | bytes 1048578
  86.6 1.8 fusion.41
  88.3 6.8 %all-to-all-start.1 = ((bf16[16,2,8192]{2,1,0:T(2,128)(2,1)}), bf16[16,2,8192]{2,1,0:T(2,128)(2,1)S(1)}, u32[]{:S(2)}, u32[]{:S(2)}) async-start(bf16[16,2,8192]{2,1,0:T(2,128)(2,1)} %reshape.508), calls=%async_computation.1 | async-start | bytes 1048576 | tf_op jit(solution)/shard_map/all_to_all | solution.py:137
  96.8 7.9 %all-to-all-done.1 = bf16[16,2,8192]{2,1,0:T(2,128)(2,1)S(1)} async-done(((bf16[16,2,8192]{2,1,0:T(2,128)(2,1)}), bf16[16,2,8192]{2,1,0:T(2,128)(2,1)S(1)}, u32[]{:S(2)}, u32[]{:S(2)}) %all-to-all-start.1) | async-done | bytes 524320 | tf_op jit(solution)/shard_map/all_to_all | solution.py:137
  104.7 4.6 all-to-all-start.2
  111.3 7.1 %all-to-all-done.2 = bf16[16,2,8192]{2,1,0:T(2,128)(2,1)} async-done(((bf16[16,2,8192]{2,1,0:T(2,128)(2,1)}), bf16[16,2,8192]{2,1,0:T(2,128)(2,1)}, u32[]{:S(2)}, u32[]{:S(2)}) %all-to-all-start.2) | async-done | bytes 524320 | tf_op jit(solution)/shard_map/all_to_all | solution.py:139
  118.4 4.2 all-to-all-start
  122.6 2.2 reshape.513
  124.9 1.9 bitcast_convert_fusion
  126.8 1.7 copy.200
  129.9 1.6 copy.201
  131.5 1.5 multiply_multiply_fusion.2
  133.9 1.9 fusion.21
  137.2 157.8 %custom-call.7 = f32[16,1,128,128]{2,3,1,0:T(8,128)} custom-call(f32[16,1,128,128]{3,2,1,0:T(8,128)S(1)} %add_bitcast_fusion), custom_call_target="InvertDiagBlocksLowerTriangular" | custom-call | tf_op jit(solution)/shard_map/jvp(vmap(jit(_solve_triangular)))/triangular_solve | solution.py:52
  295.0 6.6 %all-to-all-start.4 = ((bf16[16,2,8192]{2,1,0:T(2,128)(2,1)}), bf16[16,2,8192]{2,1,0:T(2,128)(2,1)}, u32[]{:S(2)}, u32[]{:S(2)}) async-start(bf16[16,2,8192]{2,1,0:T(2,128)(2,1)} %reshape.514), calls=%async_computation.4 | async-start | bytes 1048576 | tf_op jit(solution)/shard_map/all_to_all | solution.py:138
  301.6 2.2 reshape.511
  303.8 2.0 bitcast_convert_fusion.1
  305.8 1.7 copy.194
  308.9 1.6 copy.221
  310.5 3.5 convolution_multiply_fusion
  314.0 3.3 fusion.8
  317.3 2.3 convolution_bitcast_fusion
  319.6 3.6 reshape.515
  323.2 2.1 copy.210
  325.3 2.3 copy.211
  327.6 4.0 convolution_subtract_fusion
  331.6 2.2 fusion.16
  333.8 3.2 multiply_reduce_fusion.1
  337.0 2.1 fusion.62
  339.1 2.9 convolution_multiply_fusion.1
  342.0 2.5 fusion.37
  344.5 3.7 fusion.31
  348.2 3.1 fusion
  351.4 2.6 copy.240
  354.0 2.6 convolution_bitcast_fusion.1
  356.6 4.6 collective-permute-start
  361.2 4.9 %multiply_reduce_fusion = (f32[16,128]{1,0:T(8,128)S(1)}, f32[16,128,128]{2,1,0:T(8,128)}) fusion(f32[16,128,128]{2,1,0:T(8,128)S(1)} %copy-done.17, f32[128,128]{1,0:T(8,128)S(1)} %get-tuple-element.57, f32[16,128,128]{1,2,0:T(8,128)} %fusion.62, f32[16,1,128,128]{2,3,1,0:T(8,128)} %custom-call.7, pred[128,128]{1,0:T(8,128)(4,1)S(1)} %get-tuple-element.55), kind=kOutput, calls=%fused_computation.48 | convolution fusion | flops 403961856 | bytes 4284416 | tf_op jit(solution)/shard_map/transpose(jvp(vmap(jit(_solve_triangular))))/triangular_solve/dot.0 | solution.py:52
  366.8 6.9 %all-to-all-start.10 = ((bf16[16,128,1]{1,2,0:T(2,128)(2,1)}), bf16[16,128,1]{1,2,0:T(2,128)(2,1)S(1)}, u32[]{:S(2)}, u32[]{:S(2)}) async-start(bf16[16,128,1]{1,2,0:T(2,128)(2,1)} %copy.235), calls=%async_computation.10 | async-start | bytes 16384 | tf_op jit(solution)/shard_map/all_to_all | solution.py:161
  373.7 2.8 fusion.11
  376.5 2.3 convolution_add_fusion.3
  380.7 4.0 multiply_reduce_fusion.2
  384.8 1.4 copy.230
  386.2 3.5 multiply_convert_fusion
  390.6 6.8 %all-to-all-start.9 = ((bf16[16,128,128]{2,1,0:T(8,128)(2,1)}), bf16[16,128,128]{2,1,0:T(8,128)(2,1)}, u32[]{:S(2)}, u32[]{:S(2)}) async-start(bf16[16,128,128]{2,1,0:T(8,128)(2,1)} %copy.231), calls=%async_computation.9 | async-start | bytes 1048576 | tf_op jit(solution)/shard_map/all_to_all | solution.py:160
  397.5 2.1 add.92
  399.6 1.6 collective-permute-start.1
  401.3 3.3 fusion.4
  404.6 3.4 all-to-all-done.9
  408.1 3.6 all-to-all-start.6
  414.2 3.1 collective-permute-start.2
  417.3 4.2 all-to-all-done.6
  421.4 3.6 all-to-all-start.7
  425.0 14.9 %collective-permute-done.2 = f32[8,1,128,128]{3,0,2,1:T(8,128)S(1)} collective-permute-done((f32[8,1,128,128]{3,0,2,1:T(8,128)S(1)}, f32[8,1,128,128]{3,0,2,1:T(8,128)S(1)}, u32[]{:S(2)}, u32[]{:S(2)}) %collective-permute-start.2) | collective-permute-done | bytes 524320 | tf_op jit(solution)/shard_map/ppermute | solution.py:15
  439.9 6.6 %collective-permute-start.3 = (f32[8,1,128,128]{3,0,2,1:T(8,128)S(1)}, f32[8,1,128,128]{3,0,2,1:T(8,128)S(1)}, u32[]{:S(2)}, u32[]{:S(2)}) collective-permute-start(f32[8,1,128,128]{3,0,2,1:T(8,128)S(1)} %add.94), channel_id=1, source_target_pairs={{0,128},{16,144},{32,160},{48,176},{64,192},{80,208},{96,224},{112... | collective-permute-start | bytes 1572872 | tf_op jit(solution)/shard_map/ppermute | solution.py:15
  446.5 6.3 %all-to-all-start.8 = ((bf16[16,128,128]{2,1,0:T(8,128)(2,1)}), bf16[16,128,128]{2,1,0:T(8,128)(2,1)S(1)}, u32[]{:S(2)}, u32[]{:S(2)}) async-start(bf16[16,128,128]{2,1,0:T(8,128)(2,1)} %get-tuple-element.43), calls=%async_computation.8 | async-start | bytes 1048576 | tf_op jit(solution)/shard_map/all_to_all | solution.py:159
  457.8 5.2 %all-to-all-done.8 = bf16[16,128,128]{2,1,0:T(8,128)(2,1)S(1)} async-done(((bf16[16,128,128]{2,1,0:T(8,128)(2,1)}), bf16[16,128,128]{2,1,0:T(8,128)(2,1)S(1)}, u32[]{:S(2)}, u32[]{:S(2)}) %all-to-all-start.8) | async-done | bytes 524320 | tf_op jit(solution)/shard_map/all_to_all | solution.py:159
  464.3 4.9 %collective-permute-done.3 = f32[8,1,128,128]{3,0,2,1:T(8,128)S(1)} collective-permute-done((f32[8,1,128,128]{3,0,2,1:T(8,128)S(1)}, f32[8,1,128,128]{3,0,2,1:T(8,128)S(1)}, u32[]{:S(2)}, u32[]{:S(2)}) %collective-permute-start.3) | collective-permute-done | bytes 524320 | tf_op jit(solution)/shard_map/ppermute | solution.py:15
  (112 shorter events, 32.9 us)
Async XLA Ops:
  0.6 85.9 %copy-start = (f32[8,1,128,128]{3,2,1,0:T(8,128)S(1)}, f32[8,1,128,128]{3,2,1,0:T(8,128)}, u32[]{:S(2)}) copy-start(f32[8,1,128,128]{3,2,1,0:T(8,128)} %param.17) | copy-start | bytes 1572868
  2.0 23.7 %all-to-all-start.3 = ((bf16[1,128,16]{1,0,2:T(2,128)(2,1)}), bf16[1,128,16]{1,0,2:T(2,128)(2,1)S(1)}, u32[]{:S(2)}, u32[]{:S(2)}) async-start(bf16[1,128,16]{1,0,2:T(2,128)(2,1)} %copy.205), calls=%async_computation.3 | async-start | bytes 16384 | tf_op jit(solution)/shard_map/all_to_all | solution.py:141
  9.6 0.7 copy-start.27
  25.7 7.3 %copy-start.23 = (bf16[1,128,2048]{2,1,0:T(8,128)(2,1)S(1)}, bf16[1,128,2048]{2,1,0:T(8,128)(2,1)}, u32[]{:S(2)}) copy-start(bf16[1,128,2048]{2,1,0:T(8,128)(2,1)} %param.12) | copy-start | bytes 1572868
  25.7 62.6 %all-to-all-start.5 = ((bf16[16,2,8192]{2,1,0:T(2,128)(2,1)}), bf16[16,2,8192]{2,1,0:T(2,128)(2,1)S(1)}, u32[]{:S(2)}, u32[]{:S(2)}) async-start(bf16[16,2,8192]{2,1,0:T(2,128)(2,1)} %reshape.506), calls=%async_computation.5 | async-start | bytes 1048576 | tf_op jit(solution)/shard_map/all_to_all | solution.py:136
  45.3 1.1 copy-start.24
  58.7 1.1 copy-start.25
  72.2 0.9 copy-start.28
  72.2 1.1 copy-start.26
  88.3 16.4 %all-to-all-start.1 = ((bf16[16,2,8192]{2,1,0:T(2,128)(2,1)}), bf16[16,2,8192]{2,1,0:T(2,128)(2,1)S(1)}, u32[]{:S(2)}, u32[]{:S(2)}) async-start(bf16[16,2,8192]{2,1,0:T(2,128)(2,1)} %reshape.508), calls=%async_computation.1 | async-start | bytes 1048576 | tf_op jit(solution)/shard_map/all_to_all | solution.py:137
  104.7 13.6 %all-to-all-start.2 = ((bf16[16,2,8192]{2,1,0:T(2,128)(2,1)}), bf16[16,2,8192]{2,1,0:T(2,128)(2,1)}, u32[]{:S(2)}, u32[]{:S(2)}) async-start(bf16[16,2,8192]{2,1,0:T(2,128)(2,1)} %reshape.512), calls=%async_computation.2 | async-start | bytes 1048576 | tf_op jit(solution)/shard_map/all_to_all | solution.py:139
  118.4 176.6 %all-to-all-start = ((bf16[16,2,8192]{2,1,0:T(2,128)(2,1)}), bf16[16,2,8192]{2,1,0:T(2,128)(2,1)}, u32[]{:S(2)}, u32[]{:S(2)}) async-start(bf16[16,2,8192]{2,1,0:T(2,128)(2,1)} %reshape.510), calls=%async_computation | async-start | bytes 1048576 | tf_op jit(solution)/shard_map/all_to_all | solution.py:140
  131.4 1.5 copy-start.7
  132.9 1.0 copy-start.2
  132.9 2.9 copy-start.4
  135.8 1.0 copy-start.16
  295.0 24.6 %all-to-all-start.4 = ((bf16[16,2,8192]{2,1,0:T(2,128)(2,1)}), bf16[16,2,8192]{2,1,0:T(2,128)(2,1)}, u32[]{:S(2)}, u32[]{:S(2)}) async-start(bf16[16,2,8192]{2,1,0:T(2,128)(2,1)} %reshape.514), calls=%async_computation.4 | async-start | bytes 1048576 | tf_op jit(solution)/shard_map/all_to_all | solution.py:138
  310.5 3.5 copy-start.6
  327.6 4.0 copy-start.18
  331.6 2.2 copy-start.15
  339.1 2.9 copy-start.10
  344.5 3.7 copy-start.5
  344.5 3.7 copy-start.22
  354.0 7.2 %copy-start.17 = (f32[16,128,128]{2,1,0:T(8,128)S(1)}, f32[16,128,128]{2,1,0:T(8,128)}, u32[]{:S(2)}) copy-start(f32[16,128,128]{2,1,0:T(8,128)} %copy-done.16) | copy-start | bytes 3145732
  356.6 40.9 %collective-permute-start = (f32[8,1,128,128]{3,0,2,1:T(8,128)}, f32[8,1,128,128]{3,0,2,1:T(8,128)}, u32[]{:S(2)}, u32[]{:S(2)}) collective-permute-start(f32[8,1,128,128]{3,0,2,1:T(8,128)} %convolution_bitcast_fusion.1), channel_id=1, source_target_pairs={{0,16},{16,0},{32,48},{48,32},{64,80},{80,64},{96,112},{112,96},{1... | collective-permute-start | bytes 1572872 | tf_op jit(solution)/shard_map/ppermute | solution.py:15
  366.8 23.9 %all-to-all-start.10 = ((bf16[16,128,1]{1,2,0:T(2,128)(2,1)}), bf16[16,128,1]{1,2,0:T(2,128)(2,1)S(1)}, u32[]{:S(2)}, u32[]{:S(2)}) async-start(bf16[16,128,1]{1,2,0:T(2,128)(2,1)} %copy.235), calls=%async_computation.10 | async-start | bytes 16384 | tf_op jit(solution)/shard_map/all_to_all | solution.py:161
  373.6 2.8 copy-start.3
  373.7 2.8 copy-start.14
  373.7 2.8 copy-start.21
  376.5 2.3 copy-start.19
  378.8 1.4 copy-start.11
  378.8 1.6 copy-start.8
  378.8 1.9 copy-start.20
  380.2 4.6 copy-start.13
  390.6 10.7 %copy-start.12 = (f32[16,128,128]{1,2,0:T(8,128)S(1)}, f32[16,128,128]{1,2,0:T(8,128)}, u32[]{:S(2)}) copy-start(f32[16,128,128]{1,2,0:T(8,128)} %copy-done.11) | copy-start | bytes 3145732
  390.6 17.4 %all-to-all-start.9 = ((bf16[16,128,128]{2,1,0:T(8,128)(2,1)}), bf16[16,128,128]{2,1,0:T(8,128)(2,1)}, u32[]{:S(2)}, u32[]{:S(2)}) async-start(bf16[16,128,128]{2,1,0:T(8,128)(2,1)} %copy.231), calls=%async_computation.9 | async-start | bytes 1048576 | tf_op jit(solution)/shard_map/all_to_all | solution.py:160
  397.5 3.8 copy-start.9
  399.6 13.3 %collective-permute-start.1 = (f32[8,1,128,128]{3,0,2,1:T(8,128)}, f32[8,1,128,128]{3,0,2,1:T(8,128)}, u32[]{:S(2)}, u32[]{:S(2)}) collective-permute-start(f32[8,1,128,128]{3,0,2,1:T(8,128)} %add.92), channel_id=1, source_target_pairs={{0,32},{16,48},{32,0},{48,16},{64,96},{80,112},{96,64},{112,80},{1... | collective-permute-start | bytes 1572872 | tf_op jit(solution)/shard_map/ppermute | solution.py:15
  408.1 13.4 %all-to-all-start.6 = ((bf16[16,128,128]{1,2,0:T(8,128)(2,1)}), bf16[16,128,128]{1,2,0:T(8,128)(2,1)S(1)}, u32[]{:S(2)}, u32[]{:S(2)}) async-start(bf16[16,128,128]{1,2,0:T(8,128)(2,1)} %get-tuple-element.45), calls=%async_computation.6 | async-start | bytes 1048576 | tf_op jit(solution)/shard_map/all_to_all | solution.py:157
  414.2 25.7 %collective-permute-start.2 = (f32[8,1,128,128]{3,0,2,1:T(8,128)S(1)}, f32[8,1,128,128]{3,0,2,1:T(8,128)S(1)}, u32[]{:S(2)}, u32[]{:S(2)}) collective-permute-start(f32[8,1,128,128]{3,0,2,1:T(8,128)S(1)} %add.93), channel_id=1, source_target_pairs={{0,64},{16,80},{32,96},{48,112},{64,0},{80,16},{96,32},{112,48},{1... | collective-permute-start | bytes 1572872 | tf_op jit(solution)/shard_map/ppermute | solution.py:15
  421.4 25.1 %all-to-all-start.7 = ((bf16[16,128,128]{1,2,0:T(8,128)(2,1)}), bf16[16,128,128]{1,2,0:T(8,128)(2,1)S(1)}, u32[]{:S(2)}, u32[]{:S(2)}) async-start(bf16[16,128,128]{1,2,0:T(8,128)(2,1)} %get-tuple-element.44), calls=%async_computation.7 | async-start | bytes 1048576 | tf_op jit(solution)/shard_map/all_to_all | solution.py:158
  439.9 29.3 %collective-permute-start.3 = (f32[8,1,128,128]{3,0,2,1:T(8,128)S(1)}, f32[8,1,128,128]{3,0,2,1:T(8,128)S(1)}, u32[]{:S(2)}, u32[]{:S(2)}) collective-permute-start(f32[8,1,128,128]{3,0,2,1:T(8,128)S(1)} %add.94), channel_id=1, source_target_pairs={{0,128},{16,144},{32,160},{48,176},{64,192},{80,208},{96,224},{112... | collective-permute-start | bytes 1572872 | tf_op jit(solution)/shard_map/ppermute | solution.py:15
  446.5 16.5 %all-to-all-start.8 = ((bf16[16,128,128]{2,1,0:T(8,128)(2,1)}), bf16[16,128,128]{2,1,0:T(8,128)(2,1)S(1)}, u32[]{:S(2)}, u32[]{:S(2)}) async-start(bf16[16,128,128]{2,1,0:T(8,128)(2,1)} %get-tuple-element.43), calls=%async_computation.8 | async-start | bytes 1048576 | tf_op jit(solution)/shard_map/all_to_all | solution.py:159
  469.2 1.0 copy-start.1
